TPU v7x, 32 devices: a whole 2x2x4 slice. The times are simulated.
32 devices in a mesh: grp: 2 (over core), dp: 4 (over y, x), sp: 4 (over z).
Axes of the slice: x: 2, y: 2, z: 4, core: 2. Of those that a mesh axis runs over, the one named last changes fastest.
Arguments:
- vis: bfloat16 [512, 5120], P(('grp', 'dp', 'sp')), may hold values from -6 to 6
- merge_weight: bfloat16 [5120, 8192], P('dp', ('grp', 'sp')), may hold values from -0.078125 to 0.078125
- img_counts: int32 [32], P('dp'), may hold values from 1 to 16
- img_pos: int32 [512], P(('grp', 'dp', 'sp')), may hold values from 0 to 127, as said below
- text: bfloat16 [4096, 8192], P(('grp', 'dp', 'sp')), may hold values from -6 to 6
- cot: bfloat16 [4096, 8192], P(('grp', 'dp', 'sp')), may hold values from -6 to 6
- gain: float32 [8192], replicated, may hold values from 0.25 to 1.75
Outputs:
- vis_grad: bfloat16 [512, 5120], P(('grp', 'dp', 'sp'))
- gain_grad: float32 [8192], replicated
Inputs may be any that keep to these rules, and one draw needn't show every extreme that they name: `img_pos`: within one device's block the 16 positions are distinct. `img_counts`: the counts of one image group sum to at most 128.
All inputs are finite; a program needn't handle non-finite values.
Results may differ from a plain program's by a relative error of at most 0.014.
Values may be sent and summed in bfloat16 or wider, within the bound.
No kernel may reach another device: no remote copies, remote signals or barrier semaphores. Data moves between devices by JAX's collectives and lax.ppermute only.
A program may use at most 128 MiB of HBM per device.

v0:
```python
import jax
import jax.numpy as jnp
from jax import lax
from jax.sharding import PartitionSpec as P


def body(vis, merge_weight, img_counts, img_pos, text, cot, gain):
    rows_dev = vis.shape[0]
    tok_rows = text.shape[0]
    group_vis = lax.all_gather(vis, ("grp", "sp"), axis=0, tiled=True)
    full_weight = lax.all_gather(merge_weight, "dp", axis=0, tiled=True)
    partial_value = jnp.dot(group_vis, full_weight, preferred_element_type=jnp.float32)
    emb = lax.all_to_all(
        partial_value.astype(jnp.bfloat16), ("grp", "sp"), split_axis=0, concat_axis=1, tiled=True
    )
    total_live = jnp.sum(img_counts)
    member = lax.axis_index("grp") * lax.axis_size("sp") + lax.axis_index("sp")
    group_row = member * rows_dev + jnp.arange(rows_dev, dtype=jnp.int32)
    live = group_row < total_live
    places = jnp.arange(tok_rows, dtype=jnp.int32)
    select = (img_pos[None, :] == places[:, None]) & live[None, :]
    taken = jnp.any(select, axis=1)
    select_b = select.astype(jnp.bfloat16)
    placed = jnp.dot(select_b, emb, preferred_element_type=jnp.float32)
    hidden = jnp.where(taken[:, None], placed, text.astype(jnp.float32))
    rinv = lax.rsqrt(jnp.mean(hidden * hidden, axis=1, keepdims=True) + 1e-06)
    cotf = cot.astype(jnp.float32)
    part_gain = jnp.sum(cotf * hidden * rinv, axis=0)
    scaled = cotf * gain[None, :]
    inner = jnp.mean(scaled * hidden, axis=1, keepdims=True)
    dhid = (rinv * scaled - hidden * rinv**3 * inner).astype(jnp.bfloat16)
    demb = jnp.dot(select_b.T, dhid, preferred_element_type=jnp.float32)
    demb = jnp.where(live[:, None], demb, 0.0).astype(jnp.bfloat16)
    returned = lax.all_to_all(demb, ("grp", "sp"), split_axis=1, concat_axis=0, tiled=True)
    terms = lax.dot_general(
        returned, full_weight, (((1,), (1,)), ((), ())), preferred_element_type=jnp.float32
    )
    vis_grad = lax.psum_scatter(
        terms.astype(jnp.bfloat16), ("grp", "sp"), scatter_dimension=0, tiled=True
    )
    gain_grad = lax.psum(part_gain, ("grp", "dp", "sp"))
    return (vis_grad, gain_grad)


def solution(mesh):
    return jax.shard_map(
        body,
        mesh=mesh,
        in_specs=(
            P(("grp", "dp", "sp"), None),
            P("dp", ("grp", "sp")),
            P("dp"),
            P(("grp", "dp", "sp")),
            P(("grp", "dp", "sp"), None),
            P(("grp", "dp", "sp"), None),
            P(),
        ),
        out_specs=(P(("grp", "dp", "sp"), None), P()),
        check_vma=False,
    )
```

profile of v0, /device:TPU:0, one launch (start us, length us, event | category | flops | bytes accessed | tf_op | source)
XLA Modules:
  0.0 229.6 jit_solution(17347707635758896386)
XLA Ops:
  7.2 0.0 all-gather.3.cloned.1.call-start
  7.2 0.7 all-gather.3.cloned.1.call-update
  7.9 0.0 all-gather.5.cloned.1.call-start
  7.9 0.7 all-gather.5.cloned.1.call-update
  8.6 0.0 copy-start.4
  8.7 0.0 copy-start.3
  8.7 0.0 copy-start
  8.7 27.1 %all-gather.3.cloned.1.call-done = bf16[128,5120]{1,0:T(8,128)(2,1)} async-done(((bf16[16,5120]{1,0:T(8,128)(2,1)}), bf16[128,5120]{1,0:T(8,128)(2,1)}) %all-gather.3.cloned.1.call-update) | async-done | bytes 1310736 | tf_op jit(solution)/shard_map/all_gather | solution.py:10
  35.7 106.3 %all-gather.5.cloned.1.call-done = bf16[5120,1024]{1,0:T(8,128)(2,1)} async-done(((bf16[1280,1024]{1,0:T(8,128)(2,1)}), bf16[5120,1024]{1,0:T(8,128)(2,1)}) %all-gather.5.cloned.1.call-update) | async-done | bytes 10485776 | tf_op jit(solution)/shard_map/all_gather | solution.py:11
  142.1 6.6 %convolution_convert_fusion.1 = bf16[128,1024]{1,0:T(8,128)(2,1)} fusion(bf16[128,5120]{1,0:T(8,128)(2,1)} %all-gather.3.cloned.1.call-done, bf16[5120,1024]{1,0:T(8,128)(2,1)} %all-gather.5.cloned.1.call-done), kind=kOutput, calls=%fused_computation.14 | convolution fusion | flops 1342308352 | bytes 12058624 | tf_op jit(solution)/shard_map/dot_general | solution.py:12
  148.7 0.0 copy-start.2
  148.7 4.7 %all-to-all-start = ((bf16[8,16,1024]{2,1,0:T(8,128)(2,1)}), bf16[8,16,1024]{2,1,0:T(8,128)(2,1)S(1)}, u32[]{:S(2)}, u32[]{:S(2)}) async-start(bf16[8,16,1024]{2,1,0:T(8,128)(2,1)} %bitcast), calls=%async_computation | async-start | bytes 524288 | tf_op jit(solution)/shard_map/all_to_all | solution.py:13
  153.4 0.0 reduce-scatter.2.cloned.1.call-start
  153.5 0.0 copy-done.4
  153.5 0.6 reduce_sum.36
  154.1 0.7 add_compare_fusion
  154.8 0.0 copy-done.3
  154.8 0.1 fusion.12
  154.9 7.9 %all-to-all-done = bf16[8,16,1024]{2,1,0:T(8,128)(2,1)S(1)} async-done(((bf16[8,16,1024]{2,1,0:T(8,128)(2,1)}), bf16[8,16,1024]{2,1,0:T(8,128)(2,1)S(1)}, u32[]{:S(2)}, u32[]{:S(2)}) %all-to-all-start) | async-done | bytes 262176 | tf_op jit(solution)/shard_map/all_to_all | solution.py:13
  162.8 0.0 copy-start.1
  162.8 0.0 copy-done
  162.8 0.0 slice-start
  162.8 1.0 multiply_reduce_fusion
  163.8 0.0 copy-done.2
  163.8 0.6 copy-done.1
  164.4 0.0 slice-start.1
  164.4 1.5 fusion.7
  165.9 0.0 slice-start.2
  165.9 1.1 fusion
  167.1 11.8 %all_to_all.38 = bf16[16,8,1024]{2,0,1:T(8,128)(2,1)S(1)} all-to-all(bf16[16,8,1024]{2,0,1:T(8,128)(2,1)S(1)} %bitcast.21), channel_id=1, replica_groups=mesh['grp'=2,'dp'=4,'sp'=4] {'grp','sp'}, dimensions={1} | all-to-all | bytes 524288 | tf_op jit(solution)/shard_map/all_to_all | solution.py:34
  178.8 0.0 slice-done
  178.9 0.0 slice-done.1
  178.9 0.0 slice-done.2
  178.9 4.6 %convolution_convert_fusion = bf16[128,5120]{1,0:T(8,128)(2,1)} fusion(bf16[128,1024]{1,0:T(8,128)(2,1)S(1)} %bitcast.19, bf16[5120,1024]{1,0:T(8,128)(2,1)S(1)} %bitcast.17), kind=kOutput, calls=%fused_computation.3 | convolution fusion | flops 1342832640 | bytes 12058624 | tf_op jit(solution)/shard_map/dot_general | solution.py:35
  183.5 0.0 reduce-scatter.2.cloned.1.call-update
  183.5 39.5 %psum.7 = f32[8192]{0:T(1024)} all-reduce(f32[8192]{0:T(1024)S(1)} %get-tuple-element.2), channel_id=1, replica_groups=mesh['grp'=2,'dp'=4,'sp'=4] {'grp','dp','sp'}, use_global_device_ids=true, to_apply=%region_6.7 | all-reduce | flops 8192 | bytes 65536 | tf_op jit(solution)/shard_map/psum | solution.py:41
  223.0 0.0 reduce-scatter.2.cloned.1.call-done
  (5 shorter events, 0.1 us)
Async XLA Ops:
  7.2 28.6 %all-gather.3.cloned.1.call-start = ((), (), s32[]{:S(2)}) async-start(), calls=%async_computation.3 | async-start | bytes 1474560 | tf_op jit(solution)/shard_map/all_gather | solution.py:10
  7.9 134.2 %all-gather.5.cloned.1.call-start = ((), (), s32[]{:S(2)}) async-start(), calls=%async_computation.4 | async-start | bytes 13107200 | tf_op jit(solution)/shard_map/all_gather | solution.py:11
  8.6 144.8 %copy-start.4 = (s32[8]{0:T(128)S(1)}, s32[8]{0:T(128)}, u32[]{:S(2)}) copy-start(s32[8]{0:T(128)} %param.9) | copy-start | bytes 100
  8.7 146.1 %copy-start.3 = (s32[16]{0:T(128)S(1)}, s32[16]{0:T(128)}, u32[]{:S(2)}) copy-start(s32[16]{0:T(128)} %param.10) | copy-start | bytes 196
  8.7 154.1 %copy-start = (bf16[128,8192]{1,0:T(8,128)(2,1)S(1)}, bf16[128,8192]{1,0:T(8,128)(2,1)}, u32[]{:S(2)}) copy-start(bf16[128,8192]{1,0:T(8,128)(2,1)} %param.11) | copy-start | bytes 6291460
  148.7 15.1 %copy-start.2 = (f32[8192]{0:T(1024)S(1)}, f32[8192]{0:T(1024)}, u32[]{:S(2)}) copy-start(f32[8192]{0:T(1024)} %param.13) | copy-start | bytes 98308
  148.7 14.1 %all-to-all-start = ((bf16[8,16,1024]{2,1,0:T(8,128)(2,1)}), bf16[8,16,1024]{2,1,0:T(8,128)(2,1)S(1)}, u32[]{:S(2)}, u32[]{:S(2)}) async-start(bf16[8,16,1024]{2,1,0:T(8,128)(2,1)} %bitcast), calls=%async_computation | async-start | bytes 524288 | tf_op jit(solution)/shard_map/all_to_all | solution.py:13
  153.4 69.6 %reduce-scatter.2.cloned.1.call-start = ((), (), s32[]{:S(2)}) async-start(), calls=%async_computation.5 | async-start | bytes 1474560 | tf_op jit(solution)/shard_map/reduce_scatter | solution.py:38
  162.8 1.6 copy-start.1
  162.8 16.0 %slice-start = ((s8[10485760]{0:T(1024)(128)(4,1)}), s8[4194304]{0:T(1024)(128)(4,1)S(1)}, s32[]{:S(2)}) async-start(s8[10485760]{0:T(1024)(128)(4,1)} %bitcast.16), calls=%async_computation.6 | async-start | bytes 8388608
  164.4 14.5 %slice-start.1 = ((s8[10485760]{0:T(1024)(128)(4,1)}), s8[4194304]{0:T(1024)(128)(4,1)S(1)}, s32[]{:S(2)}) async-start(s8[10485760]{0:T(1024)(128)(4,1)} %bitcast.16), calls=%async_computation.7 | async-start | bytes 8388608
  165.9 13.0 %slice-start.2 = ((s8[10485760]{0:T(1024)(128)(4,1)}), s8[2097152]{0:T(1024)(128)(4,1)S(1)}, s32[]{:S(2)}) async-start(s8[10485760]{0:T(1024)(128)(4,1)} %bitcast.16), calls=%async_computation.8 | async-start | bytes 4194304
Sparse Core Ops, SparseCore 0:
  9.6 26.1 all-gather.2
  37.6 104.4 all-gather.4
  183.6 34.8 reduce-scatter.1
where the time goes:
time: 230 us
  waiting for transfers between devices  143 us (62%)
  blocking collectives  51.3 us (22%)
  between operations  13.9 us (6%)
  matrix products  13.4 us (6%)
  starting transfers between devices  4.85 us (2%)
  other arithmetic  2.91 us (1%)
    all_gather x1, waiting for transfers between devices, body(): full_weight = lax.all_gather(merge_weight, 'dp', axis=0, tiled=True)  106 us
    psum x1, blocking collectives, body(): gain_grad = lax.psum(part_gain, ('grp', 'dp', 'sp'))  39.5 us
    all_gather x1, waiting for transfers between devices, body(): group_vis = lax.all_gather(vis, ('grp', 'sp'), axis=0, tiled=True)  27.1 us
    all_to_all x1, blocking collectives, body(): lax.all_to_all(demb, ('grp', 'sp'), split_axis=1, concat_axis=0, tiled=True)  11.8 us
    all_to_all x1, waiting for transfers between devices, body(): lax.all_to_all(partial_value.astype(jnp.bfloat16), ('grp', 'sp'), split_a...  7.9 us
    dot_general x1, matrix products, body(): jnp.dot(group_vis, full_weight, preferred_element_type=jnp.float32)  6.62 us
    all_to_all x1, starting transfers between devices, body(): lax.all_to_all(partial_value.astype(jnp.bfloat16), ('grp', 'sp'), split_a...  4.74 us
    dot_general x1, matrix products, body(): lax.dot_general(returned, full_weight, (((1,), (1,)), ((), ())), preferre...  4.62 us
  transfers between devices with their start and end apart: 4, of which 3 were waited for; matrix products, arithmetic and copies ran while one was open for 1% of the time, Pallas kernels for 0%

commit v1 on v0

v1 whole, which is shorter than its diff:
```python
import jax
import jax.numpy as jnp
from jax import lax
from jax.sharding import PartitionSpec as P

F32 = jnp.float32
BF16 = jnp.bfloat16
DIRECT = 8


def pairs(n, k):
    return [(i, i ^ k) for i in range(n)]


def relative(x, me):
    n = x.shape[0]
    return jnp.stack([lax.dynamic_index_in_dim(x, me ^ k, 0, keepdims=False) for k in range(n)])


def swap(blocks, axis):
    n = len(blocks)
    if n <= DIRECT:
        return [blocks[0]] + [lax.ppermute(blocks[k], axis, pairs(n, k)) for k in range(1, n)]
    me = lax.axis_index(axis)
    index = me ^ jnp.arange(n)
    sent = jnp.take(jnp.stack(blocks), index, axis=0)
    got = lax.all_to_all(sent, axis, 0, 0, tiled=True)
    got = jnp.take(got, index, axis=0)
    return [got[k] for k in range(n)]


def share(x, axis):
    n = lax.axis_size(axis)
    if n <= DIRECT:
        return [x] + [lax.ppermute(x, axis, pairs(n, k)) for k in range(1, n)]
    me = lax.axis_index(axis)
    got = jnp.take(lax.all_gather(x, axis), me ^ jnp.arange(n), axis=0)
    return [got[k] for k in range(n)]


def body(vis, weight, img_counts, img_pos, text, cot, gain):
    n_g, n_d, n_s = (lax.axis_size(a) for a in ("grp", "dp", "sp"))
    g, d, s = (lax.axis_index(a) for a in ("grp", "dp", "sp"))
    rb = vis.shape[0]
    toks, dm = text.shape
    dc, kc = weight.shape
    rows = n_g * n_s * rb

    own = relative(vis.reshape(rb, n_d, dc).transpose(1, 0, 2), d)
    mine = jnp.stack(swap([own[k] for k in range(n_d)], "dp"))
    along = share(mine, "sp")
    pieces = [share(p, "grp") for p in along]
    every = jnp.stack([jnp.stack([pieces[j][i] for j in range(n_s)]) for i in range(n_g)])
    every = every.transpose(2, 0, 1, 3, 4).reshape(n_d, rows, dc)
    part = [jnp.dot(every[k], weight, preferred_element_type=F32).astype(BF16) for k in range(n_d)]
    got = swap(part, "dp")
    emb = sum(p.astype(F32) for p in got).astype(BF16).astype(F32)

    total = jnp.sum(img_counts)
    group_row = (g * n_s + s) * rb + jnp.arange(rb, dtype=jnp.int32)
    live = group_row < total
    places = jnp.arange(toks, dtype=jnp.int32)
    select = (img_pos[None, :] == places[:, None]) & live[None, :]
    taken = jnp.any(select, axis=1)
    picked = jnp.dot(select.astype(BF16).T, cot, preferred_element_type=F32).astype(BF16)
    picked = picked.reshape(rb, n_g, n_s, kc).transpose(2, 1, 0, 3)
    picked = relative(picked, s)
    seen = swap([picked[k] for k in range(n_s)], "sp")
    seen = relative(jnp.stack(seen, axis=1), g)
    seen = jnp.stack(swap([seen[k] for k in range(n_g)], "grp"))
    cotf = seen.reshape(rows, kc).astype(F32)

    textf = text.astype(F32)
    keep = jnp.where(taken[:, None], 0.0, lax.rsqrt(jnp.mean(textf * textf, axis=1, keepdims=True) + 1e-06))
    text_gain = jnp.sum(cot.astype(F32) * textf * keep, axis=0)
    text_gain = relative(text_gain.reshape(n_g, n_s, kc), g)
    text_gain = relative(text_gain.transpose(1, 0, 2), s)

    gk = lax.dynamic_slice_in_dim(gain, (g * n_s + s) * kc, kc)
    scaled = cotf * gk[None, :]
    stats = jnp.stack([jnp.sum(emb * emb, axis=1), jnp.sum(scaled * emb, axis=1)])
    n_stat = 2 * rows
    near = jnp.concatenate([stats.reshape(-1), text_gain[:, 1].reshape(-1)])
    far = lax.ppermute(near, "grp", pairs(n_g, 1))
    far_stats = far[:n_stat].reshape(2, n_g, n_s, rb)[:, ::-1]
    stats = stats.reshape(2, n_g, n_s, rb) + far_stats
    text_gain = text_gain[:, 0] + far[n_stat:].reshape(n_s, kc)
    sent = [jnp.concatenate([stats.reshape(-1), text_gain[k]]) for k in range(n_s)]
    got = swap(sent, "sp")
    stats = sum(
        got[k][:n_stat].reshape(2, n_g, n_s, rb)[:, :, jnp.array([j ^ k for j in range(n_s)])] for k in range(n_s)
    )
    text_gain = sum(got[k][n_stat:] for k in range(n_s))
    stats = stats.reshape(2, rows, 1) / dm
    rinv = lax.rsqrt(stats[0] + 1e-06)
    inner = stats[1]

    row = (
        ((g ^ jnp.arange(n_g))[:, None, None] * n_s + (s ^ jnp.arange(n_s))[None, :, None]) * rb
        + jnp.arange(rb)[None, None, :]
    ).reshape(rows, 1)
    alive = row < total
    demb = jnp.where(alive, rinv * scaled - emb * rinv**3 * inner, 0.0).astype(BF16)
    gain_part = text_gain + jnp.sum(jnp.where(alive, cotf * emb * rinv, 0.0), axis=0)

    rows_k = share(demb, "dp")
    gain_k = sum(share(gain_part, "dp"))
    back = jnp.stack(
        [
            lax.dot_general(r, weight, (((1,), (1,)), ((), ())), preferred_element_type=F32).astype(BF16)
            for r in rows_k
        ]
    ).reshape(n_d, n_g, n_s, rb, dc)
    got = lax.ppermute(back[:, 1], "grp", pairs(n_g, 1))
    half = (back[:, 0].astype(F32) + got.astype(F32)).astype(BF16)
    got = swap([half[:, k] for k in range(n_s)], "sp")
    done = sum(x.astype(F32) for x in got).astype(BF16)
    got = relative(jnp.stack(swap([done[k] for k in range(n_d)], "dp")), d)
    vis_grad = got.transpose(1, 0, 2).reshape(rb, n_d * dc)

    gains = relative(jnp.stack(share(gain_k, "sp")), s)
    gains = relative(jnp.stack(share(gains, "grp")), g)
    return vis_grad, gains.reshape(dm)


def solution(mesh):
    return jax.shard_map(
        body,
        mesh=mesh,
        in_specs=(
            P(("grp", "dp", "sp"), None),
            P("dp", ("grp", "sp")),
            P("dp"),
            P(("grp", "dp", "sp")),
            P(("grp", "dp", "sp"), None),
            P(("grp", "dp", "sp"), None),
            P(),
        ),
        out_specs=(P(("grp", "dp", "sp"), None), P()),
        check_vma=False,
    )
```

time: 230 us -> 125 us (0.54)
  waiting for transfers between devices: 143 us -> 51.1 us
  blocking collectives: 51.3 us -> 0 us
  starting transfers between devices: 4.85 us -> 42.7 us
  between operations: 13.9 us -> 1.27 us
  local copies, waits for them, and re-layouts: 0.62 us -> 8.06 us
  other arithmetic: 2.91 us -> 9.7 us
    all_gather x2 -> x0, waiting for transfers between devices: 133 us -> none  [the longest x1 106 us: body(): full_weight = lax.all_gather(merge_weight, 'dp', axis=0, tiled=True)]
    ppermute x0 -> x38, waiting for transfers between devices: none -> 51.1 us  [the longest x17 27.2 us: share(): return [x] + [lax.ppermute(x, axis, pairs(n, k)) for k in range(1, n)]]
    ppermute x0 -> x38, starting transfers between devices: none -> 42.7 us  [the longest x19 26 us: swap(): lax.ppermute(blocks[k], axis, pairs(n, k))]
    psum x1 -> x0, blocking collectives: 39.5 us -> none  [body(): gain_grad = lax.psum(part_gain, ('grp', 'dp', 'sp'))]
    all_to_all x1 -> x0, blocking collectives: 11.8 us -> none  [body(): lax.all_to_all(demb, ('grp', 'sp'), split_axis=1, concat_axis=0, tiled=True)]
    all_to_all x1 -> x0, waiting for transfers between devices: 7.9 us -> none  [body(): lax.all_to_all(partial_value.astype(jnp.bfloat16), ('grp', 'sp'), split_a...]
    all_to_all x1 -> x0, starting transfers between devices: 4.74 us -> none  [body(): lax.all_to_all(partial_value.astype(jnp.bfloat16), ('grp', 'sp'), split_a...]
    reduce_sum x2 -> x4, other arithmetic: 2.15 us -> 6.26 us  [the longest x1 2.35 us: body(): text_gain = jnp.sum(cot.astype(F32) * textf * keep, axis=0)]
  transfers between devices with their start and end apart: 4 -> 38, of which waited for: 3 -> 23; matrix products, arithmetic and copies ran while one was open for 1% -> 17% of each run, Pallas kernels for 0% -> 0%
where the time goes in v1:
time: 125 us; the launch traced here: 124 us
  waiting for transfers between devices  51.1 us (41%)
  starting transfers between devices  42.7 us (34%)
  matrix products  11.6 us (9%)
  other arithmetic  9.7 us (8%)
  local copies, waits for them, and re-layouts  8.06 us (6%)
  between operations  1.27 us (1%)
    ppermute x17, waiting for transfers between devices, share(): return [x] + [lax.ppermute(x, axis, pairs(n, k)) for k in range(1, n)]  27.2 us
    ppermute x19, starting transfers between devices, swap(): lax.ppermute(blocks[k], axis, pairs(n, k))  26 us
    ppermute x19, waiting for transfers between devices, swap(): lax.ppermute(blocks[k], axis, pairs(n, k))  22.9 us
    ppermute x17, starting transfers between devices, share(): return [x] + [lax.ppermute(x, axis, pairs(n, k)) for k in range(1, n)]  16.6 us
    dot_general x4, matrix products, body(): jnp.dot(every[k], weight, preferred_element_type=F32).astype(BF16)  5.57 us
    dot_general x4, matrix products, body(): lax.dot_general(r, weight, (((1,), (1,)), ((), ())), preferred_element_ty...  4.01 us
  transfers between devices with their start and end apart: 38, of which 23 were waited for; matrix products, arithmetic and copies ran while one was open for 17% of the time, Pallas kernels for 0%

profile of v1, /device:TPU:0, one launch (start us, length us, event | category | flops | bytes accessed | tf_op | source)
XLA Modules:
  0.0 124.5 jit_solution(13821782987223648699)
XLA Ops:
  0.7 1.2 reshape.272
  2.2 3.0 %collective-permute-start = (bf16[16,1280]{1,0:T(8,128)(2,1)S(1)}, bf16[16,1280]{1,0:T(8,128)(2,1)S(1)}, u32[]{:S(2)}, u32[]{:S(2)}) collective-permute-start(bf16[16,1280]{1,0:T(8,128)(2,1)S(1)} %bitcast.193), channel_id=1, source_target_pairs={{0,4},{4,0},{8,12},{12,8},{1,5},{5,1},{9,13},{13,9},{2,6},{6,2},{1... | collective-permute-start | bytes 122888 | tf_op jit(solution)/shard_map/ppermute | solution.py:23
  5.3 1.5 %collective-permute-start.1 = (bf16[16,1280]{1,0:T(8,128)(2,1)S(1)}, bf16[16,1280]{1,0:T(8,128)(2,1)S(1)}, u32[]{:S(2)}, u32[]{:S(2)}) collective-permute-start(bf16[16,1280]{1,0:T(8,128)(2,1)S(1)} %bitcast.192), channel_id=1, source_target_pairs={{0,8},{4,12},{8,0},{12,4},{1,9},{5,13},{9,1},{13,5},{2,10},{6,14},... | collective-permute-start | bytes 122888 | tf_op jit(solution)/shard_map/ppermute | solution.py:23
  6.9 1.3 %reduce_sum.54 = s32[]{:T(128)} reduce(s32[8]{0:T(128)} %param.13, s32[]{:T(128)} %constant.105.clone.1), dimensions={0}, to_apply=%region_0.1 | reduce | flops 7 | bytes 40 | tf_op jit(solution)/shard_map/reduce_sum | solution.py:59
  8.8 2.0 %convolution_convert_fusion = bf16[16,8192]{1,0:T(8,128)(2,1)S(1)} fusion(bf16[128,8192]{1,0:T(8,128)(2,1)} %param.16, s32[16]{0:T(128)} %param.14, pred[16]{0:T(512)(128)(4,1)S(1)} %add_compare_fusion.1), kind=kOutput, calls=%fused_computation.4 | convolution fusion | flops 33689600 | bytes 2359376 | tf_op jit(solution)/shard_map/dot_general | solution.py:65
  11.7 2.0 %collective-permute-start.13 = (bf16[2,16,1024]{2,1,0:T(8,128)(2,1)S(1)}, bf16[2,16,1024]{2,1,0:T(8,128)(2,1)S(1)}, u32[]{:S(2)}, u32[]{:S(2)}) collective-permute-start(bf16[2,16,1024]{2,1,0:T(8,128)(2,1)S(1)} %bitcast.183), channel_id=1, source_target_pairs={{0,1},{1,0},{2,3},{3,2},{4,5},{5,4},{6,7},{7,6},{8,9},{9,8},{10,11... | collective-permute-start | bytes 196616 | tf_op jit(solution)/shard_map/ppermute | solution.py:23
  13.8 2.7 %collective-permute-start.14 = (bf16[2,16,1024]{2,1,0:T(8,128)(2,1)S(1)}, bf16[2,16,1024]{2,1,0:T(8,128)(2,1)S(1)}, u32[]{:S(2)}, u32[]{:S(2)}) collective-permute-start(bf16[2,16,1024]{2,1,0:T(8,128)(2,1)S(1)} %bitcast.182), channel_id=1, source_target_pairs={{0,2},{1,3},{2,0},{3,1},{4,6},{5,7},{6,4},{7,5},{8,10},{9,11},{10,... | collective-permute-start | bytes 196616 | tf_op jit(solution)/shard_map/ppermute | solution.py:23
  16.6 2.2 %fusion.2 = f32[128]{0:T(128)S(1)} fusion(bf16[128,8192]{1,0:T(8,128)(2,1)} %param.15), kind=kLoop, calls=%fused_computation.9 | loop fusion | flops 3145600 | bytes 2097664 | tf_op jit(solution)/shard_map/reduce_sum | solution.py:74
  18.8 2.3 %fusion.1 = f32[8192]{0:T(1024)S(1)} fusion(bf16[128,8192]{1,0:T(8,128)(2,1)} %param.15, bf16[128,8192]{1,0:T(8,128)(2,1)S(1)} %copy-done.1, f32[128]{0:T(128)S(1)} %rsqrt_select_fusion), kind=kLoop, calls=%fused_computation.8 | loop fusion | flops 5234688 | bytes 4227584 | tf_op jit(solution)/shard_map/reduce_sum | solution.py:75
  23.1 0.9 collective-permute-start.3
  24.1 3.5 %collective-permute-start.4 = (bf16[4,16,1280]{2,1,0:T(8,128)(2,1)S(1)}, bf16[4,16,1280]{2,1,0:T(8,128)(2,1)S(1)}, u32[]{:S(2)}, u32[]{:S(2)}) collective-permute-start(bf16[4,16,1280]{2,1,0:T(8,128)(2,1)S(1)} %get-tuple-element.29), channel_id=1, source_target_pairs={{0,2},{1,3},{2,0},{3,1},{4,6},{5,7},{6,4},{7,5},{8,10},{9,11},{10,... | collective-permute-start | bytes 491528 | tf_op jit(solution)/shard_map/ppermute | solution.py:35
  27.6 1.5 %collective-permute-done.15 = bf16[2,16,1024]{2,1,0:T(8,128)(2,1)S(1)} collective-permute-done((bf16[2,16,1024]{2,1,0:T(8,128)(2,1)S(1)}, bf16[2,16,1024]{2,1,0:T(8,128)(2,1)S(1)}, u32[]{:S(2)}, u32[]{:S(2)}) %collective-permute-start.15) | collective-permute-done | bytes 65568 | tf_op jit(solution)/shard_map/ppermute | solution.py:23
  29.3 9.8 %collective-permute-done.4 = bf16[4,16,1280]{2,1,0:T(8,128)(2,1)S(1)} collective-permute-done((bf16[4,16,1280]{2,1,0:T(8,128)(2,1)S(1)}, bf16[4,16,1280]{2,1,0:T(8,128)(2,1)S(1)}, u32[]{:S(2)}, u32[]{:S(2)}) %collective-permute-start.4) | collective-permute-done | bytes 163872 | tf_op jit(solution)/shard_map/ppermute | solution.py:35
  41.3 1.2 convolution_convert_fusion.7
  42.5 1.5 %collective-permute-start.10 = (bf16[128,1024]{1,0:T(8,128)(2,1)}, bf16[128,1024]{1,0:T(8,128)(2,1)}, u32[]{:S(2)}, u32[]{:S(2)}) collective-permute-start(bf16[128,1024]{1,0:T(8,128)(2,1)} %convolution_convert_fusion.7), channel_id=1, source_target_pairs={{0,4},{4,0},{8,12},{12,8},{1,5},{5,1},{9,13},{13,9},{2,6},{6,2},{1... | collective-permute-start | bytes 786440 | tf_op jit(solution)/shard_map/ppermute | solution.py:23
  44.0 1.2 convolution_convert_fusion.6
  45.2 1.5 %collective-permute-start.11 = (bf16[128,1024]{1,0:T(8,128)(2,1)}, bf16[128,1024]{1,0:T(8,128)(2,1)}, u32[]{:S(2)}, u32[]{:S(2)}) collective-permute-start(bf16[128,1024]{1,0:T(8,128)(2,1)} %convolution_convert_fusion.6), channel_id=1, source_target_pairs={{0,8},{4,12},{8,0},{12,4},{1,9},{5,13},{9,1},{13,5},{2,10},{6,14},... | collective-permute-start | bytes 786440 | tf_op jit(solution)/shard_map/ppermute | solution.py:23
  46.8 1.2 convolution_convert_fusion.5
  49.3 2.8 %collective-permute-done.10 = bf16[128,1024]{1,0:T(8,128)(2,1)} collective-permute-done((bf16[128,1024]{1,0:T(8,128)(2,1)}, bf16[128,1024]{1,0:T(8,128)(2,1)}, u32[]{:S(2)}, u32[]{:S(2)}) %collective-permute-start.10) | collective-permute-done | bytes 262176 | tf_op jit(solution)/shard_map/ppermute | solution.py:23
  52.0 7.3 %collective-permute-done.11 = bf16[128,1024]{1,0:T(8,128)(2,1)} collective-permute-done((bf16[128,1024]{1,0:T(8,128)(2,1)}, bf16[128,1024]{1,0:T(8,128)(2,1)}, u32[]{:S(2)}, u32[]{:S(2)}) %collective-permute-start.11) | collective-permute-done | bytes 262176 | tf_op jit(solution)/shard_map/ppermute | solution.py:23
  59.4 1.9 %fusion.9 = (f32[128]{0:T(128)S(1)}, f32[128]{0:T(128)S(1)}, bf16[128,1024]{1,0:T(8,128)(2,1)S(1)}) fusion(f32[1024]{0:T(1024)S(1)} %dynamic_slice.88, bf16[2,4,16,1024]{3,2,1,0:T(8,128)(2,1)S(1)} %pad_maximum_fusion.2, bf16[128,1024]{1,0:T(8,128)(2,1)} %collective-permute-done.12, bf16[128,1024]{1,0:T(8,128)(2,1)} %collective-permute-done.11, ...), kind=kOutput, calls=%fused_computation.36 | convolution fusion | flops 337641216 | bytes 4264960 | tf_op jit(solution)/shard_map/dot_general | solution.py:55
  61.6 1.0 collective-permute-done.17
  62.9 2.6 %collective-permute-start.18 = (f32[1280]{0:T(1024)S(1)}, f32[1280]{0:T(1024)S(1)}, u32[]{:S(2)}, u32[]{:S(2)}) collective-permute-start(f32[1280]{0:T(1024)S(1)} %get-tuple-element.54), channel_id=1, source_target_pairs={{0,1},{1,0},{2,3},{3,2},{4,5},{5,4},{6,7},{7,6},{8,9},{9,8},{10,11... | collective-permute-start | bytes 15368 | tf_op jit(solution)/shard_map/ppermute | solution.py:23
  65.9 2.0 %collective-permute-start.20 = (f32[1280]{0:T(1024)S(1)}, f32[1280]{0:T(1024)S(1)}, u32[]{:S(2)}, u32[]{:S(2)}) collective-permute-start(f32[1280]{0:T(1024)S(1)} %get-tuple-element.56), channel_id=1, source_target_pairs={{0,3},{1,2},{2,1},{3,0},{4,7},{5,6},{6,5},{7,4},{8,11},{9,10},{10,... | collective-permute-start | bytes 15368 | tf_op jit(solution)/shard_map/ppermute | solution.py:23
  68.7 1.3 %collective-permute-done.19 = f32[1280]{0:T(1024)S(1)} collective-permute-done((f32[1280]{0:T(1024)S(1)}, f32[1280]{0:T(1024)S(1)}, u32[]{:S(2)}, u32[]{:S(2)}) %collective-permute-start.19) | collective-permute-done | bytes 5152 | tf_op jit(solution)/shard_map/ppermute | solution.py:23
  70.1 1.2 collective-permute-done.20
  74.3 1.6 %collective-permute-start.22 = (bf16[128,1024]{1,0:T(8,128)(2,1)S(1)}, bf16[128,1024]{1,0:T(8,128)(2,1)S(1)}, u32[]{:S(2)}, u32[]{:S(2)}) collective-permute-start(bf16[128,1024]{1,0:T(8,128)(2,1)S(1)} %get-tuple-element.13), channel_id=1, source_target_pairs={{0,8},{4,12},{8,0},{12,4},{1,9},{5,13},{9,1},{13,5},{2,10},{6,14},... | collective-permute-start | bytes 786440 | tf_op jit(solution)/shard_map/ppermute | solution.py:35
  75.9 1.4 %collective-permute-start.23 = (bf16[128,1024]{1,0:T(8,128)(2,1)S(1)}, bf16[128,1024]{1,0:T(8,128)(2,1)S(1)}, u32[]{:S(2)}, u32[]{:S(2)}) collective-permute-start(bf16[128,1024]{1,0:T(8,128)(2,1)S(1)} %get-tuple-element.13), channel_id=1, source_target_pairs={{0,12},{4,8},{8,4},{12,0},{1,13},{5,9},{9,5},{13,1},{2,14},{6,10},... | collective-permute-start | bytes 786440 | tf_op jit(solution)/shard_map/ppermute | solution.py:35
  77.3 1.0 convolution_convert_fusion.4
  78.3 4.7 %collective-permute-done.21 = bf16[128,1024]{1,0:T(8,128)(2,1)S(1)} collective-permute-done((bf16[128,1024]{1,0:T(8,128)(2,1)S(1)}, bf16[128,1024]{1,0:T(8,128)(2,1)S(1)}, u32[]{:S(2)}, u32[]{:S(2)}) %collective-permute-start.21) | collective-permute-done | bytes 262176 | tf_op jit(solution)/shard_map/ppermute | solution.py:35
  83.0 1.0 convolution_convert_fusion.3
  84.0 1.7 %collective-permute-done.22 = bf16[128,1024]{1,0:T(8,128)(2,1)S(1)} collective-permute-done((bf16[128,1024]{1,0:T(8,128)(2,1)S(1)}, bf16[128,1024]{1,0:T(8,128)(2,1)S(1)}, u32[]{:S(2)}, u32[]{:S(2)}) %collective-permute-start.22) | collective-permute-done | bytes 262176 | tf_op jit(solution)/shard_map/ppermute | solution.py:35
  85.7 1.0 convolution_convert_fusion.2
  87.4 1.0 convolution_convert_fusion.1
  88.7 1.9 %collective-permute-start.31 = (f32[1024]{0:T(1024)S(1)}, f32[1024]{0:T(1024)S(1)}, u32[]{:S(2)}, u32[]{:S(2)}) collective-permute-start(f32[1024]{0:T(1024)S(1)} %fusion.34), channel_id=1, source_target_pairs={{0,4},{4,0},{8,12},{12,8},{1,5},{5,1},{9,13},{13,9},{2,6},{6,2},{1... | collective-permute-start | bytes 12296 | tf_op jit(solution)/shard_map/ppermute | solution.py:35
  90.6 1.5 %collective-permute-start.32 = (f32[1024]{0:T(1024)S(1)}, f32[1024]{0:T(1024)S(1)}, u32[]{:S(2)}, u32[]{:S(2)}) collective-permute-start(f32[1024]{0:T(1024)S(1)} %fusion.34), channel_id=1, source_target_pairs={{0,8},{4,12},{8,0},{12,4},{1,9},{5,13},{9,1},{13,5},{2,10},{6,14},... | collective-permute-start | bytes 12296 | tf_op jit(solution)/shard_map/ppermute | solution.py:35
  92.4 1.8 %collective-permute-done.32 = f32[1024]{0:T(1024)S(1)} collective-permute-done((f32[1024]{0:T(1024)S(1)}, f32[1024]{0:T(1024)S(1)}, u32[]{:S(2)}, u32[]{:S(2)}) %collective-permute-start.32) | collective-permute-done | bytes 4128 | tf_op jit(solution)/shard_map/ppermute | solution.py:35
  94.2 2.4 %collective-permute-done.33 = f32[1024]{0:T(1024)S(1)} collective-permute-done((f32[1024]{0:T(1024)S(1)}, f32[1024]{0:T(1024)S(1)}, u32[]{:S(2)}, u32[]{:S(2)}) %collective-permute-start.33) | collective-permute-done | bytes 4128 | tf_op jit(solution)/shard_map/ppermute | solution.py:35
  96.7 2.4 %collective-permute-start.35 = (f32[1024]{0:T(1024)S(1)}, f32[1024]{0:T(1024)S(1)}, u32[]{:S(2)}, u32[]{:S(2)}) collective-permute-start(f32[1024]{0:T(1024)S(1)} %add_add_fusion), channel_id=1, source_target_pairs={{0,2},{1,3},{2,0},{3,1},{4,6},{5,7},{6,4},{7,5},{8,10},{9,11},{10,... | collective-permute-start | bytes 12296 | tf_op jit(solution)/shard_map/ppermute | solution.py:35
  99.2 1.8 %collective-permute-start.36 = (f32[1024]{0:T(1024)S(1)}, f32[1024]{0:T(1024)S(1)}, u32[]{:S(2)}, u32[]{:S(2)}) collective-permute-start(f32[1024]{0:T(1024)S(1)} %add_add_fusion), channel_id=1, source_target_pairs={{0,3},{1,2},{2,1},{3,0},{4,7},{5,6},{6,5},{7,4},{8,11},{9,10},{10,... | collective-permute-start | bytes 12296 | tf_op jit(solution)/shard_map/ppermute | solution.py:35
  101.2 3.4 %collective-permute-done.36 = f32[1024]{0:T(1024)S(1)} collective-permute-done((f32[1024]{0:T(1024)S(1)}, f32[1024]{0:T(1024)S(1)}, u32[]{:S(2)}, u32[]{:S(2)}) %collective-permute-start.36) | collective-permute-done | bytes 4128 | tf_op jit(solution)/shard_map/ppermute | solution.py:35
  105.0 2.4 %collective-permute-start.26 = (bf16[4,16,1280]{2,1,0:T(8,128)(2,1)S(1)}, bf16[4,16,1280]{2,1,0:T(8,128)(2,1)S(1)}, u32[]{:S(2)}, u32[]{:S(2)}) collective-permute-start(bf16[4,16,1280]{2,1,0:T(8,128)(2,1)S(1)} %get-tuple-element.11), channel_id=1, source_target_pairs={{0,2},{1,3},{2,0},{3,1},{4,6},{5,7},{6,4},{7,5},{8,10},{9,11},{10,... | collective-permute-start | bytes 491528 | tf_op jit(solution)/shard_map/ppermute | solution.py:23
  107.4 2.0 %collective-permute-start.27 = (bf16[4,16,1280]{2,1,0:T(8,128)(2,1)S(1)}, bf16[4,16,1280]{2,1,0:T(8,128)(2,1)S(1)}, u32[]{:S(2)}, u32[]{:S(2)}) collective-permute-start(bf16[4,16,1280]{2,1,0:T(8,128)(2,1)S(1)} %get-tuple-element.10), channel_id=1, source_target_pairs={{0,3},{1,2},{2,1},{3,0},{4,7},{5,6},{6,5},{7,4},{8,11},{9,10},{10,... | collective-permute-start | bytes 491528 | tf_op jit(solution)/shard_map/ppermute | solution.py:23
  109.5 1.2 collective-permute-done.37
  110.7 2.4 %collective-permute-done.25 = bf16[4,16,1280]{2,1,0:T(8,128)(2,1)S(1)} collective-permute-done((bf16[4,16,1280]{2,1,0:T(8,128)(2,1)S(1)}, bf16[4,16,1280]{2,1,0:T(8,128)(2,1)S(1)}, u32[]{:S(2)}, u32[]{:S(2)}) %collective-permute-start.25) | collective-permute-done | bytes 163872 | tf_op jit(solution)/shard_map/ppermute | solution.py:23
  113.1 4.6 %collective-permute-done.26 = bf16[4,16,1280]{2,1,0:T(8,128)(2,1)S(1)} collective-permute-done((bf16[4,16,1280]{2,1,0:T(8,128)(2,1)S(1)}, bf16[4,16,1280]{2,1,0:T(8,128)(2,1)S(1)}, u32[]{:S(2)}, u32[]{:S(2)}) %collective-permute-start.26) | collective-permute-done | bytes 163872 | tf_op jit(solution)/shard_map/ppermute | solution.py:23
  118.8 2.6 %collective-permute-start.30 = (bf16[16,1280]{1,0:T(8,128)(2,1)S(1)}, bf16[16,1280]{1,0:T(8,128)(2,1)S(1)}, u32[]{:S(2)}, u32[]{:S(2)}) collective-permute-start(bf16[16,1280]{1,0:T(8,128)(2,1)S(1)} %get-tuple-element.25), channel_id=1, source_target_pairs={{0,12},{4,8},{8,4},{12,0},{1,13},{5,9},{9,5},{13,1},{2,14},{6,10},... | collective-permute-start | bytes 122888 | tf_op jit(solution)/shard_map/ppermute | solution.py:23
  122.5 1.3 %collective-permute-done.30 = bf16[16,1280]{1,0:T(8,128)(2,1)S(1)} collective-permute-done((bf16[16,1280]{1,0:T(8,128)(2,1)S(1)}, bf16[16,1280]{1,0:T(8,128)(2,1)S(1)}, u32[]{:S(2)}, u32[]{:S(2)}) %collective-permute-start.30) | collective-permute-done | bytes 40992 | tf_op jit(solution)/shard_map/ppermute | solution.py:23
  (147 shorter events, 17.2 us)
Async XLA Ops:
  0.6 40.7 %copy-start = (bf16[1280,1024]{1,0:T(8,128)(2,1)S(1)}, bf16[1280,1024]{1,0:T(8,128)(2,1)}, u32[]{:S(2)}) copy-start(bf16[1280,1024]{1,0:T(8,128)(2,1)} %param.12) | copy-start | bytes 7864324
  1.9 14.6 %copy-start.5 = (s32[16]{0:T(128)S(1)}, s32[16]{0:T(128)}, u32[]{:S(2)}) copy-start(s32[16]{0:T(128)} %param.14) | copy-start | bytes 196
  2.2 20.0 %collective-permute-start = (bf16[16,1280]{1,0:T(8,128)(2,1)S(1)}, bf16[16,1280]{1,0:T(8,128)(2,1)S(1)}, u32[]{:S(2)}, u32[]{:S(2)}) collective-permute-start(bf16[16,1280]{1,0:T(8,128)(2,1)S(1)} %bitcast.193), channel_id=1, source_target_pairs={{0,4},{4,0},{8,12},{12,8},{1,5},{5,1},{9,13},{13,9},{2,6},{6,2},{1... | collective-permute-start | bytes 122888 | tf_op jit(solution)/shard_map/ppermute | solution.py:23
  5.3 17.0 %collective-permute-start.1 = (bf16[16,1280]{1,0:T(8,128)(2,1)S(1)}, bf16[16,1280]{1,0:T(8,128)(2,1)S(1)}, u32[]{:S(2)}, u32[]{:S(2)}) collective-permute-start(bf16[16,1280]{1,0:T(8,128)(2,1)S(1)} %bitcast.192), channel_id=1, source_target_pairs={{0,8},{4,12},{8,0},{12,4},{1,9},{5,13},{9,1},{13,5},{2,10},{6,14},... | collective-permute-start | bytes 122888 | tf_op jit(solution)/shard_map/ppermute | solution.py:23
  6.8 15.5 %collective-permute-start.2 = (bf16[16,1280]{1,0:T(8,128)(2,1)S(1)}, bf16[16,1280]{1,0:T(8,128)(2,1)}, u32[]{:S(2)}, u32[]{:S(2)}) collective-permute-start(bf16[16,1280]{1,0:T(8,128)(2,1)S(1)} %bitcast.194), channel_id=1, source_target_pairs={{0,12},{4,8},{8,4},{12,0},{1,13},{5,9},{9,5},{13,1},{2,14},{6,10},... | collective-permute-start | bytes 122888 | tf_op jit(solution)/shard_map/ppermute | solution.py:23
  11.7 15.8 %collective-permute-start.13 = (bf16[2,16,1024]{2,1,0:T(8,128)(2,1)S(1)}, bf16[2,16,1024]{2,1,0:T(8,128)(2,1)S(1)}, u32[]{:S(2)}, u32[]{:S(2)}) collective-permute-start(bf16[2,16,1024]{2,1,0:T(8,128)(2,1)S(1)} %bitcast.183), channel_id=1, source_target_pairs={{0,1},{1,0},{2,3},{3,2},{4,5},{5,4},{6,7},{7,6},{8,9},{9,8},{10,11... | collective-permute-start | bytes 196616 | tf_op jit(solution)/shard_map/ppermute | solution.py:23
  13.8 13.8 %collective-permute-start.14 = (bf16[2,16,1024]{2,1,0:T(8,128)(2,1)S(1)}, bf16[2,16,1024]{2,1,0:T(8,128)(2,1)S(1)}, u32[]{:S(2)}, u32[]{:S(2)}) collective-permute-start(bf16[2,16,1024]{2,1,0:T(8,128)(2,1)S(1)} %bitcast.182), channel_id=1, source_target_pairs={{0,2},{1,3},{2,0},{3,1},{4,6},{5,7},{6,4},{7,5},{8,10},{9,11},{10,... | collective-permute-start | bytes 196616 | tf_op jit(solution)/shard_map/ppermute | solution.py:23
  16.4 2.3 %copy-start.1 = (bf16[128,8192]{1,0:T(8,128)(2,1)S(1)}, bf16[128,8192]{1,0:T(8,128)(2,1)}, u32[]{:S(2)}) copy-start(bf16[128,8192]{1,0:T(8,128)(2,1)} %param.16) | copy-start | bytes 6291460
  22.2 6.9 %collective-permute-start.15 = (bf16[2,16,1024]{2,1,0:T(8,128)(2,1)S(1)}, bf16[2,16,1024]{2,1,0:T(8,128)(2,1)S(1)}, u32[]{:S(2)}, u32[]{:S(2)}) collective-permute-start(bf16[2,16,1024]{2,1,0:T(8,128)(2,1)S(1)} %bitcast.184), channel_id=1, source_target_pairs={{0,3},{1,2},{2,1},{3,0},{4,7},{5,6},{6,5},{7,4},{8,11},{9,10},{10,... | collective-permute-start | bytes 196616 | tf_op jit(solution)/shard_map/ppermute | solution.py:23
  23.1 16.5 %collective-permute-start.3 = (bf16[4,16,1280]{2,1,0:T(8,128)(2,1)S(1)}, bf16[4,16,1280]{2,1,0:T(8,128)(2,1)S(1)}, u32[]{:S(2)}, u32[]{:S(2)}) collective-permute-start(bf16[4,16,1280]{2,1,0:T(8,128)(2,1)S(1)} %get-tuple-element.29), channel_id=1, source_target_pairs={{0,1},{1,0},{2,3},{3,2},{4,5},{5,4},{6,7},{7,6},{8,9},{9,8},{10,11... | collective-permute-start | bytes 491528 | tf_op jit(solution)/shard_map/ppermute | solution.py:35
  24.1 15.0 %collective-permute-start.4 = (bf16[4,16,1280]{2,1,0:T(8,128)(2,1)S(1)}, bf16[4,16,1280]{2,1,0:T(8,128)(2,1)S(1)}, u32[]{:S(2)}, u32[]{:S(2)}) collective-permute-start(bf16[4,16,1280]{2,1,0:T(8,128)(2,1)S(1)} %get-tuple-element.29), channel_id=1, source_target_pairs={{0,2},{1,3},{2,0},{3,1},{4,6},{5,7},{6,4},{7,5},{8,10},{9,11},{10,... | collective-permute-start | bytes 491528 | tf_op jit(solution)/shard_map/ppermute | solution.py:35
  27.5 11.5 %collective-permute-start.5 = (bf16[4,16,1280]{2,1,0:T(8,128)(2,1)S(1)}, bf16[4,16,1280]{2,1,0:T(8,128)(2,1)S(1)}, u32[]{:S(2)}, u32[]{:S(2)}) collective-permute-start(bf16[4,16,1280]{2,1,0:T(8,128)(2,1)S(1)} %get-tuple-element.29), channel_id=1, source_target_pairs={{0,3},{1,2},{2,1},{3,0},{4,7},{5,6},{6,5},{7,4},{8,11},{9,10},{10,... | collective-permute-start | bytes 491528 | tf_op jit(solution)/shard_map/ppermute | solution.py:35
  27.6 12.2 %collective-permute-start.6 = (bf16[4,16,1280]{2,1,0:T(8,128)(2,1)S(1)}, bf16[4,16,1280]{2,1,0:T(8,128)(2,1)S(1)}, u32[]{:S(2)}, u32[]{:S(2)}) collective-permute-start(bf16[4,16,1280]{2,1,0:T(8,128)(2,1)S(1)} %get-tuple-element.29), channel_id=1, source_target_pairs={{0,16},{16,0},{1,17},{17,1},{2,18},{18,2},{3,19},{19,3},{4,20},{20... | collective-permute-start | bytes 491528 | tf_op jit(solution)/shard_map/ppermute | solution.py:35
  29.2 20.0 %collective-permute-start.16 = (bf16[4,16,1024]{2,1,0:T(8,128)(2,1)S(1)}, bf16[4,16,1024]{2,1,0:T(8,128)(2,1)S(1)}, u32[]{:S(2)}, u32[]{:S(2)}) collective-permute-start(bf16[4,16,1024]{2,1,0:T(8,128)(2,1)S(1)} %get-tuple-element.15), channel_id=1, source_target_pairs={{0,16},{16,0},{1,17},{17,1},{2,18},{18,2},{3,19},{19,3},{4,20},{20... | collective-permute-start | bytes 393224 | tf_op jit(solution)/shard_map/ppermute | solution.py:23
  39.1 1.4 %collective-permute-start.8 = (bf16[4,16,1280]{2,1,0:T(8,128)(2,1)S(1)}, bf16[4,16,1280]{2,1,0:T(8,128)(2,1)S(1)}, u32[]{:S(2)}, u32[]{:S(2)}) collective-permute-start(bf16[4,16,1280]{2,1,0:T(8,128)(2,1)S(1)} %collective-permute-done.4), channel_id=1, source_target_pairs={{0,16},{16,0},{1,17},{17,1},{2,18},{18,2},{3,19},{19,3},{4,20},{20... | collective-permute-start | bytes 491528 | tf_op jit(solution)/shard_map/ppermute | solution.py:35
  39.1 1.6 %collective-permute-start.9 = (bf16[4,16,1280]{2,1,0:T(8,128)(2,1)S(1)}, bf16[4,16,1280]{2,1,0:T(8,128)(2,1)S(1)}, u32[]{:S(2)}, u32[]{:S(2)}) collective-permute-start(bf16[4,16,1280]{2,1,0:T(8,128)(2,1)S(1)} %collective-permute-done.5), channel_id=1, source_target_pairs={{0,16},{16,0},{1,17},{17,1},{2,18},{18,2},{3,19},{19,3},{4,20},{20... | collective-permute-start | bytes 491528 | tf_op jit(solution)/shard_map/ppermute | solution.py:35
  39.6 1.4 %collective-permute-start.7 = (bf16[4,16,1280]{2,1,0:T(8,128)(2,1)S(1)}, bf16[4,16,1280]{2,1,0:T(8,128)(2,1)S(1)}, u32[]{:S(2)}, u32[]{:S(2)}) collective-permute-start(bf16[4,16,1280]{2,1,0:T(8,128)(2,1)S(1)} %collective-permute-done.3), channel_id=1, source_target_pairs={{0,16},{16,0},{1,17},{17,1},{2,18},{18,2},{3,19},{19,3},{4,20},{20... | collective-permute-start | bytes 491528 | tf_op jit(solution)/shard_map/ppermute | solution.py:35
  42.5 9.5 %collective-permute-start.10 = (bf16[128,1024]{1,0:T(8,128)(2,1)}, bf16[128,1024]{1,0:T(8,128)(2,1)}, u32[]{:S(2)}, u32[]{:S(2)}) collective-permute-start(bf16[128,1024]{1,0:T(8,128)(2,1)} %convolution_convert_fusion.7), channel_id=1, source_target_pairs={{0,4},{4,0},{8,12},{12,8},{1,5},{5,1},{9,13},{13,9},{2,6},{6,2},{1... | collective-permute-start | bytes 786440 | tf_op jit(solution)/shard_map/ppermute | solution.py:23
  44.0 4.4 %copy-start.4 = (s32[4]{0:T(128)S(1)}, s32[4]{0:T(128)}, u32[]{:S(2)}) copy-start(s32[4]{0:T(128)} %constant.134) | copy-start | bytes 52
  44.0 5.2 %copy-start.3 = (s32[4]{0:T(128)S(1)}, s32[4]{0:T(128)}, u32[]{:S(2)}) copy-start(s32[4]{0:T(128)} %constant.135) | copy-start | bytes 52
  45.2 14.1 %collective-permute-start.11 = (bf16[128,1024]{1,0:T(8,128)(2,1)}, bf16[128,1024]{1,0:T(8,128)(2,1)}, u32[]{:S(2)}, u32[]{:S(2)}) collective-permute-start(bf16[128,1024]{1,0:T(8,128)(2,1)} %convolution_convert_fusion.6), channel_id=1, source_target_pairs={{0,8},{4,12},{8,0},{12,4},{1,9},{5,13},{9,1},{13,5},{2,10},{6,14},... | collective-permute-start | bytes 786440 | tf_op jit(solution)/shard_map/ppermute | solution.py:23
  48.0 13.4 %copy-start.2 = (s32[4]{0:T(128)S(1)}, s32[4]{0:T(128)}, u32[]{:S(2)}) copy-start(s32[4]{0:T(128)} %constant.136) | copy-start | bytes 52
  48.0 11.4 %collective-permute-start.12 = (bf16[128,1024]{1,0:T(8,128)(2,1)}, bf16[128,1024]{1,0:T(8,128)(2,1)}, u32[]{:S(2)}, u32[]{:S(2)}) collective-permute-start(bf16[128,1024]{1,0:T(8,128)(2,1)} %convolution_convert_fusion.5), channel_id=1, source_target_pairs={{0,12},{4,8},{8,4},{12,0},{1,13},{5,9},{9,5},{13,1},{2,14},{6,10},... | collective-permute-start | bytes 786440 | tf_op jit(solution)/shard_map/ppermute | solution.py:23
  61.3 1.3 %collective-permute-start.17 = (f32[4352]{0:T(1024)S(1)}, f32[4352]{0:T(1024)S(1)}, u32[]{:S(2)}, u32[]{:S(2)}) collective-permute-start(f32[4352]{0:T(1024)S(1)} %pad_maximum_fusion.6), channel_id=1, source_target_pairs={{0,16},{16,0},{1,17},{17,1},{2,18},{18,2},{3,19},{19,3},{4,20},{20... | collective-permute-start | bytes 52232 | tf_op jit(solution)/shard_map/ppermute | solution.py:84
  62.9 5.7 %collective-permute-start.18 = (f32[1280]{0:T(1024)S(1)}, f32[1280]{0:T(1024)S(1)}, u32[]{:S(2)}, u32[]{:S(2)}) collective-permute-start(f32[1280]{0:T(1024)S(1)} %get-tuple-element.54), channel_id=1, source_target_pairs={{0,1},{1,0},{2,3},{3,2},{4,5},{5,4},{6,7},{7,6},{8,9},{9,8},{10,11... | collective-permute-start | bytes 15368 | tf_op jit(solution)/shard_map/ppermute | solution.py:23
  65.4 4.5 %collective-permute-start.19 = (f32[1280]{0:T(1024)S(1)}, f32[1280]{0:T(1024)S(1)}, u32[]{:S(2)}, u32[]{:S(2)}) collective-permute-start(f32[1280]{0:T(1024)S(1)} %get-tuple-element.55), channel_id=1, source_target_pairs={{0,2},{1,3},{2,0},{3,1},{4,6},{5,7},{6,4},{7,5},{8,10},{9,11},{10,... | collective-permute-start | bytes 15368 | tf_op jit(solution)/shard_map/ppermute | solution.py:23
  65.9 5.4 %collective-permute-start.20 = (f32[1280]{0:T(1024)S(1)}, f32[1280]{0:T(1024)S(1)}, u32[]{:S(2)}, u32[]{:S(2)}) collective-permute-start(f32[1280]{0:T(1024)S(1)} %get-tuple-element.56), channel_id=1, source_target_pairs={{0,3},{1,2},{2,1},{3,0},{4,7},{5,6},{6,5},{7,4},{8,11},{9,10},{10,... | collective-permute-start | bytes 15368 | tf_op jit(solution)/shard_map/ppermute | solution.py:23
  73.8 9.2 %collective-permute-start.21 = (bf16[128,1024]{1,0:T(8,128)(2,1)S(1)}, bf16[128,1024]{1,0:T(8,128)(2,1)S(1)}, u32[]{:S(2)}, u32[]{:S(2)}) collective-permute-start(bf16[128,1024]{1,0:T(8,128)(2,1)S(1)} %get-tuple-element.13), channel_id=1, source_target_pairs={{0,4},{4,0},{8,12},{12,8},{1,5},{5,1},{9,13},{13,9},{2,6},{6,2},{1... | collective-permute-start | bytes 786440 | tf_op jit(solution)/shard_map/ppermute | solution.py:35
  74.3 11.5 %collective-permute-start.22 = (bf16[128,1024]{1,0:T(8,128)(2,1)S(1)}, bf16[128,1024]{1,0:T(8,128)(2,1)S(1)}, u32[]{:S(2)}, u32[]{:S(2)}) collective-permute-start(bf16[128,1024]{1,0:T(8,128)(2,1)S(1)} %get-tuple-element.13), channel_id=1, source_target_pairs={{0,8},{4,12},{8,0},{12,4},{1,9},{5,13},{9,1},{13,5},{2,10},{6,14},... | collective-permute-start | bytes 786440 | tf_op jit(solution)/shard_map/ppermute | solution.py:35
  75.9 11.5 %collective-permute-start.23 = (bf16[128,1024]{1,0:T(8,128)(2,1)S(1)}, bf16[128,1024]{1,0:T(8,128)(2,1)S(1)}, u32[]{:S(2)}, u32[]{:S(2)}) collective-permute-start(bf16[128,1024]{1,0:T(8,128)(2,1)S(1)} %get-tuple-element.13), channel_id=1, source_target_pairs={{0,12},{4,8},{8,4},{12,0},{1,13},{5,9},{9,5},{13,1},{2,14},{6,10},... | collective-permute-start | bytes 786440 | tf_op jit(solution)/shard_map/ppermute | solution.py:35
  88.6 16.1 %collective-permute-start.24 = (bf16[4,4,16,1280]{3,2,1,0:T(8,128)(2,1)S(1)}, bf16[4,4,16,1280]{3,2,1,0:T(8,128)(2,1)S(1)}, u32[]{:S(2)}, u32[]{:S(2)}) collective-permute-start(bf16[4,4,16,1280]{3,2,1,0:T(8,128)(2,1)S(1)} %slice_bitcast_fusion), channel_id=1, source_target_pairs={{0,16},{16,0},{1,17},{17,1},{2,18},{18,2},{3,19},{19,3},{4,20},{20... | collective-permute-start | bytes 1966088 | tf_op jit(solution)/shard_map/ppermute | solution.py:114
  88.7 3.7 %collective-permute-start.31 = (f32[1024]{0:T(1024)S(1)}, f32[1024]{0:T(1024)S(1)}, u32[]{:S(2)}, u32[]{:S(2)}) collective-permute-start(f32[1024]{0:T(1024)S(1)} %fusion.34), channel_id=1, source_target_pairs={{0,4},{4,0},{8,12},{12,8},{1,5},{5,1},{9,13},{13,9},{2,6},{6,2},{1... | collective-permute-start | bytes 12296 | tf_op jit(solution)/shard_map/ppermute | solution.py:35
  90.6 3.6 %collective-permute-start.32 = (f32[1024]{0:T(1024)S(1)}, f32[1024]{0:T(1024)S(1)}, u32[]{:S(2)}, u32[]{:S(2)}) collective-permute-start(f32[1024]{0:T(1024)S(1)} %fusion.34), channel_id=1, source_target_pairs={{0,8},{4,12},{8,0},{12,4},{1,9},{5,13},{9,1},{13,5},{2,10},{6,14},... | collective-permute-start | bytes 12296 | tf_op jit(solution)/shard_map/ppermute | solution.py:35
  92.1 4.5 %collective-permute-start.33 = (f32[1024]{0:T(1024)S(1)}, f32[1024]{0:T(1024)S(1)}, u32[]{:S(2)}, u32[]{:S(2)}) collective-permute-start(f32[1024]{0:T(1024)S(1)} %fusion.34), channel_id=1, source_target_pairs={{0,12},{4,8},{8,4},{12,0},{1,13},{5,9},{9,5},{13,1},{2,14},{6,10},... | collective-permute-start | bytes 12296 | tf_op jit(solution)/shard_map/ppermute | solution.py:35
  96.6 4.4 %collective-permute-start.34 = (f32[1024]{0:T(1024)S(1)}, f32[1024]{0:T(1024)S(1)}, u32[]{:S(2)}, u32[]{:S(2)}) collective-permute-start(f32[1024]{0:T(1024)S(1)} %add_add_fusion), channel_id=1, source_target_pairs={{0,1},{1,0},{2,3},{3,2},{4,5},{5,4},{6,7},{7,6},{8,9},{9,8},{10,11... | collective-permute-start | bytes 12296 | tf_op jit(solution)/shard_map/ppermute | solution.py:35
  96.7 4.5 %collective-permute-start.35 = (f32[1024]{0:T(1024)S(1)}, f32[1024]{0:T(1024)S(1)}, u32[]{:S(2)}, u32[]{:S(2)}) collective-permute-start(f32[1024]{0:T(1024)S(1)} %add_add_fusion), channel_id=1, source_target_pairs={{0,2},{1,3},{2,0},{3,1},{4,6},{5,7},{6,4},{7,5},{8,10},{9,11},{10,... | collective-permute-start | bytes 12296 | tf_op jit(solution)/shard_map/ppermute | solution.py:35
  99.2 5.5 %collective-permute-start.36 = (f32[1024]{0:T(1024)S(1)}, f32[1024]{0:T(1024)S(1)}, u32[]{:S(2)}, u32[]{:S(2)}) collective-permute-start(f32[1024]{0:T(1024)S(1)} %add_add_fusion), channel_id=1, source_target_pairs={{0,3},{1,2},{2,1},{3,0},{4,7},{5,6},{6,5},{7,4},{8,11},{9,10},{10,... | collective-permute-start | bytes 12296 | tf_op jit(solution)/shard_map/ppermute | solution.py:35
  104.9 8.2 %collective-permute-start.25 = (bf16[4,16,1280]{2,1,0:T(8,128)(2,1)S(1)}, bf16[4,16,1280]{2,1,0:T(8,128)(2,1)S(1)}, u32[]{:S(2)}, u32[]{:S(2)}) collective-permute-start(bf16[4,16,1280]{2,1,0:T(8,128)(2,1)S(1)} %get-tuple-element.9), channel_id=1, source_target_pairs={{0,1},{1,0},{2,3},{3,2},{4,5},{5,4},{6,7},{7,6},{8,9},{9,8},{10,11... | collective-permute-start | bytes 491528 | tf_op jit(solution)/shard_map/ppermute | solution.py:23
  105.0 12.7 %collective-permute-start.26 = (bf16[4,16,1280]{2,1,0:T(8,128)(2,1)S(1)}, bf16[4,16,1280]{2,1,0:T(8,128)(2,1)S(1)}, u32[]{:S(2)}, u32[]{:S(2)}) collective-permute-start(bf16[4,16,1280]{2,1,0:T(8,128)(2,1)S(1)} %get-tuple-element.11), channel_id=1, source_target_pairs={{0,2},{1,3},{2,0},{3,1},{4,6},{5,7},{6,4},{7,5},{8,10},{9,11},{10,... | collective-permute-start | bytes 491528 | tf_op jit(solution)/shard_map/ppermute | solution.py:23
  107.4 10.4 %collective-permute-start.27 = (bf16[4,16,1280]{2,1,0:T(8,128)(2,1)S(1)}, bf16[4,16,1280]{2,1,0:T(8,128)(2,1)S(1)}, u32[]{:S(2)}, u32[]{:S(2)}) collective-permute-start(bf16[4,16,1280]{2,1,0:T(8,128)(2,1)S(1)} %get-tuple-element.10), channel_id=1, source_target_pairs={{0,3},{1,2},{2,1},{3,0},{4,7},{5,6},{6,5},{7,4},{8,11},{9,10},{10,... | collective-permute-start | bytes 491528 | tf_op jit(solution)/shard_map/ppermute | solution.py:23
  109.4 1.2 %collective-permute-start.37 = (f32[4,1024]{1,0:T(4,128)S(1)}, f32[4,1024]{1,0:T(4,128)S(1)}, u32[]{:S(2)}, u32[]{:S(2)}) collective-permute-start(f32[4,1024]{1,0:T(4,128)S(1)} %get-tuple-element.42), channel_id=1, source_target_pairs={{0,16},{16,0},{1,17},{17,1},{2,18},{18,2},{3,19},{19,3},{4,20},{20... | collective-permute-start | bytes 49160 | tf_op jit(solution)/shard_map/ppermute | solution.py:35
  117.9 4.2 %collective-permute-start.28 = (bf16[16,1280]{1,0:T(8,128)(2,1)S(1)}, bf16[16,1280]{1,0:T(8,128)(2,1)S(1)}, u32[]{:S(2)}, u32[]{:S(2)}) collective-permute-start(bf16[16,1280]{1,0:T(8,128)(2,1)S(1)} %get-tuple-element.27), channel_id=1, source_target_pairs={{0,4},{4,0},{8,12},{12,8},{1,5},{5,1},{9,13},{13,9},{2,6},{6,2},{1... | collective-permute-start | bytes 122888 | tf_op jit(solution)/shard_map/ppermute | solution.py:23
  118.5 4.0 %collective-permute-start.29 = (bf16[16,1280]{1,0:T(8,128)(2,1)S(1)}, bf16[16,1280]{1,0:T(8,128)(2,1)S(1)}, u32[]{:S(2)}, u32[]{:S(2)}) collective-permute-start(bf16[16,1280]{1,0:T(8,128)(2,1)S(1)} %get-tuple-element.26), channel_id=1, source_target_pairs={{0,8},{4,12},{8,0},{12,4},{1,9},{5,13},{9,1},{13,5},{2,10},{6,14},... | collective-permute-start | bytes 122888 | tf_op jit(solution)/shard_map/ppermute | solution.py:23
  118.8 4.9 %collective-permute-start.30 = (bf16[16,1280]{1,0:T(8,128)(2,1)S(1)}, bf16[16,1280]{1,0:T(8,128)(2,1)S(1)}, u32[]{:S(2)}, u32[]{:S(2)}) collective-permute-start(bf16[16,1280]{1,0:T(8,128)(2,1)S(1)} %get-tuple-element.25), channel_id=1, source_target_pairs={{0,12},{4,8},{8,4},{12,0},{1,13},{5,9},{9,5},{13,1},{2,14},{6,10},... | collective-permute-start | bytes 122888 | tf_op jit(solution)/shard_map/ppermute | solution.py:23
